TPU v7x, 128 devices: a whole 4x4x4 slice. The times are simulated.
128 devices in a mesh: row: 4 (over y), col: 32 (over x, z, core).
Axes of the slice: x: 4, y: 4, z: 4, core: 2. Of those that a mesh axis runs over, the one named last changes fastest.
Arguments:
- frontal: bfloat16 [16384, 49152], P('row', 'col')
- sample_cols: bfloat16 [49152, 64], P(('col', 'row')), may hold values from -6 to 6
- leaf_first: int32 [256], replicated, may hold values from 0 to 16352, as said below
- leaf_owner: int32 [256], replicated, may hold values from 0 to 31, as said below
- skeleton: int32 [256, 16], replicated, may hold values from 0 to 16383, as said below
Outputs:
- owner_samples: float32 [256, 8192], P('row', 'col')
- interp: float32 [64, 8192], P('row', 'col')
- worst: float32 [1], replicated
Inputs may be any that keep to these rules, and one draw needn't show every extreme that they name: `leaf_first`: leaves are consecutive and ascending; the first leaf of row group g starts at g * 4096; each row group has 64 leaves whose sizes are 1 to 5 times 32, in 16 runs of four consecutive leaves of together 256 rows. `leaf_owner`: each run of four leaves is owned by at most two devices of the group; the leaves one device owns in its group hold at most 256 rows and number at most 4; in every row group some device reaches both. Each leaf's skeleton rows are 16 distinct rows of that leaf, ascending.
All inputs are finite; a program needn't handle non-finite values.
Results may differ from a plain program's by a relative error of at most 0.0003.
Values may be sent and summed in bfloat16 or wider, within the bound.
A program may use at most 64 MiB of HBM per device.

v0:
```python
import jax
import jax.numpy as jnp
from jax import lax
from jax.sharding import PartitionSpec as P

LEAF_MOST = 4


def leaf_index(values, leaf_first):
    return jnp.sum((leaf_first[None, :] <= values[:, None]).astype(jnp.int32), axis=1) - 1


def local(frontal, sample_cols, leaf_first, leaf_owner, skeleton):
    highest = lax.Precision.HIGHEST
    group_rows, width = frontal.shape
    samples_count = sample_cols.shape[1]
    skel_count = skeleton.shape[1]
    leaves = leaf_first.shape[0]
    n_col = lax.axis_size("col")
    n_row = lax.axis_size("row")
    per_group = leaves // n_row
    total_rows = group_rows * n_row
    share_rows = group_rows // n_col
    capacity = 2 * share_rows
    row_pos = lax.axis_index("row")
    col_pos = lax.axis_index("col")
    rows = row_pos * group_rows + jnp.arange(group_rows, dtype=jnp.int32)
    row_leaf = leaf_index(rows, leaf_first)
    zero_entry = jnp.zeros((), frontal.dtype)
    piece = lax.all_gather(sample_cols, "row", axis=0, tiled=True)
    span = piece.shape[0]
    cols = col_pos * width + jnp.arange(span, dtype=jnp.int32)
    col_leaf = leaf_index(cols, leaf_first)
    same = (row_leaf[:, None] == col_leaf[None, :]) & (cols[None, :] < total_rows)
    kept = jnp.where(same, zero_entry, frontal)
    partial_value = jnp.dot(kept, piece, preferred_element_type=jnp.float32)
    ends = jnp.concatenate([leaf_first[1:], jnp.full((1,), total_rows, jnp.int32)])
    sizes = ends - leaf_first
    leaf_ids = jnp.arange(leaves, dtype=jnp.int32)
    group_of = leaf_ids // per_group
    own_hot = (leaf_owner[:, None] == jnp.arange(n_col, dtype=jnp.int32)[None, :]).astype(jnp.int32)
    weighted = (own_hot * sizes[:, None]).reshape(n_row, per_group, n_col)
    before = (jnp.cumsum(weighted, axis=1) - weighted).reshape(leaves, n_col)
    offset = jnp.sum(before * own_hot, axis=1)
    counted = own_hot.reshape(n_row, per_group, n_col)
    earlier = (jnp.cumsum(counted, axis=1) - counted).reshape(leaves, n_col)
    rank = jnp.sum(earlier * own_hot, axis=1)
    owned = (leaf_owner == col_pos) & (group_of == row_pos)
    slots = jnp.arange(capacity, dtype=jnp.int32)
    slot_hit = (
        owned[None, :]
        & (offset[None, :] <= slots[:, None])
        & (slots[:, None] < (offset + sizes)[None, :])
    )
    slot_hit_int = slot_hit.astype(jnp.int32)
    valid = jnp.any(slot_hit, axis=1)
    local_row = (
        jnp.sum(slot_hit_int * (leaf_first[None, :] + slots[:, None] - offset[None, :]), axis=1)
        - row_pos * group_rows
    )
    local_row = jnp.clip(local_row, 0, group_rows - 1)
    valid_float = valid[:, None].astype(jnp.float32)
    summed = lax.psum(partial_value, "col")
    mine = jnp.take(summed, local_row, axis=0) * valid_float
    select = owned[None, :] & (rank[None, :] == jnp.arange(LEAF_MOST, dtype=jnp.int32)[:, None])
    select_int = select.astype(jnp.int32)
    present = jnp.any(select, axis=1).astype(jnp.float32)
    skel_slot = jnp.sum(
        select_int[:, :, None] * (offset[:, None] + skeleton - leaf_first[:, None])[None, :, :],
        axis=1,
    )
    skel_slot = jnp.clip(skel_slot, 0, capacity - 1)
    picked = jnp.take(mine, skel_slot.reshape(-1), axis=0).reshape(
        LEAF_MOST, skel_count, samples_count
    )
    picked = picked * present[:, None, None]
    identity = jnp.eye(skel_count, dtype=jnp.float32)
    gram = jnp.einsum("kjp,kip->kji", picked, picked, precision=highest)
    gram = gram + (1.0 - present)[:, None, None] * identity[None, :, :]
    factor = jnp.linalg.cholesky(gram)
    inverse = jax.vmap(lambda lower: jax.scipy.linalg.cho_solve((lower, True), identity))(factor)
    slot_rank = jnp.sum(slot_hit_int * rank[None, :], axis=1)
    slot_pick = (
        (slot_rank[:, None] == jnp.arange(LEAF_MOST, dtype=jnp.int32)[None, :]) & valid[:, None]
    ).astype(jnp.float32)
    project = jnp.einsum("sp,kjp->skj", mine, picked, precision=highest)
    coeff_all = jnp.einsum("skj,kji->ski", project, inverse, precision=highest)
    coeff = jnp.sum(coeff_all * slot_pick[:, :, None], axis=1)
    rebuilt_all = jnp.einsum("ski,kip->skp", coeff_all, picked, precision=highest)
    rebuilt = jnp.sum(rebuilt_all * slot_pick[:, :, None], axis=1)
    resid = mine - rebuilt
    err = jnp.sum(slot_pick * jnp.sum(resid * resid, axis=1)[:, None], axis=0)
    norm = jnp.sum(slot_pick * jnp.sum(mine * mine, axis=1)[:, None], axis=0)
    ratio = jnp.sqrt(err) / jnp.sqrt(norm + 1e-06)
    local_worst = jnp.max(jnp.where(present > 0.5, ratio, 0.0)).reshape(1)
    worst = lax.pmax(local_worst, ("row", "col"))
    return (mine.T, coeff.T, worst)


def solution(mesh):
    return jax.shard_map(
        local,
        mesh=mesh,
        in_specs=(P("row", "col"), P(("col", "row"), None), P(), P(), P()),
        out_specs=(P("row", "col"), P("row", "col"), P()),
        check_vma=False,
    )
```

profile of v0, /device:TPU:1, one launch (start us, length us, event | category | flops | bytes accessed | tf_op | source)
XLA Modules:
  0.0 230.8 jit_solution(219416975980167111)
XLA Ops:
  7.2 0.0 all-reduce.2.cloned.1.call-start
  7.2 10.9 %all_gather.3 = bf16[1536,64]{0,1:T(8,128)(2,1)S(1)} all-gather(bf16[384,64]{0,1:T(8,128)(2,1)} %param.6), channel_id=1, replica_groups=mesh['row'=4,'col'=32] {'row'}, dimensions={0}, use_global_device_ids=true | all-gather | bytes 245760 | tf_op jit(solution)/shard_map/all_gather | solution.py:30
  18.2 1.2 convert_reduce_fusion.1
  19.4 2.0 convert_reduce_fusion
  21.4 0.0 copy-start
  21.4 0.0 copy-start.1
  21.4 7.9 %fusion = f32[4096,64]{0,1:T(8,128)} fusion(bf16[1536,64]{0,1:T(8,128)(2,1)S(1)} %all_gather.3, bf16[4096,1536]{1,0:T(8,128)(2,1)} %param.5, s32[1536]{0:T(1024)S(1)} %broadcast_add_fusion.1, s32[4096]{0:T(1024)S(1)} %broadcast_add_fusion, pred[1536]{0:T(1024)(128)(4,1)S(1)} %broadcast_compare_fusion), kind=kOutput, calls=%fused_computation.3 | convolution fusion | flops 824180736 | bytes 13852160 | tf_op jit(solution)/shard_map/dot_general | solution.py:36
  29.3 0.0 all-reduce.2.cloned.1.call-update
  29.3 0.1 slice.21
  29.4 0.1 eq.93
  29.5 0.1 fusion.10
  29.6 0.1 add_subtract_fusion.1
  29.7 0.1 mul.125
  29.8 0.1 fusion.11
  29.9 0.1 reduce_window_sum.18
  30.0 0.1 reduce_window_sum.17
  30.2 0.3 select_reduce_fusion.2
  30.5 0.1 le.64
  30.6 0.1 eq.100
  30.7 0.1 fusion.19
  30.8 0.2 select_reduce_fusion
  31.1 0.1 fusion.33
  31.3 0.1 multiply_reduce_fusion.3
  31.5 0.1 min.25
  31.6 108.0 %all-reduce.2.cloned.1.call-done = f32[4096,64]{0,1:T(8,128)} async-done(((f32[4096,64]{0,1:T(8,128)}), f32[4096,64]{0,1:T(8,128)}) %all-reduce.2.cloned.1.call-update) | async-done | bytes 1048592 | tf_op jit(solution)/shard_map/psum | solution.py:63
  139.6 1.8 copy.23
  141.4 0.7 gather_fusion
  142.1 0.1 fusion.48
  142.3 0.1 select_multiply_fusion
  142.4 0.6 gather_fusion.1
  143.0 0.3 fusion.18
  143.3 0.3 fusion.8
  143.6 0.7 copy.28
  144.3 0.1 copy.24
  144.4 0.1 fusion.17
  144.5 5.9 %custom-call.11 = f32[4,16,16]{2,1,0:T(8,128)S(1)} custom-call(f32[4,16,16]{2,1,0:T(8,128)S(1)} %fusion.17), custom_call_target="Cholesky" | custom-call | tf_op jit(solution)/shard_map/jit(cholesky)/cholesky | solution.py:80
  150.4 0.1 compare_reduce_fusion
  150.5 0.1 select_bitcast_fusion
  150.6 4.9 %custom-call.12 = f32[4,1,16,16]{2,3,1,0:T(8,128)S(1)} custom-call(f32[4,1,16,16]{3,2,1,0:T(8,128)S(1)} %select_bitcast_fusion), custom_call_target="InvertDiagBlocksLowerTriangular" | custom-call | tf_op jit(solution)/shard_map/vmap(jit(_cho_solve))/triangular_solve | solution.py:81
  155.5 0.3 fusion.14
  155.8 0.2 fusion.12
  156.0 0.8 multiply_reduce_fusion.2
  156.8 0.5 fusion.5
  157.3 0.1 copy.27
  157.4 0.3 multiply_reduce_fusion.1
  157.7 0.2 select_reduce_fusion.6
  157.8 0.6 fusion.36
  158.4 65.5 %pmax.7 = f32[1]{0:T(128)} all-reduce(f32[1]{0:T(128)} %bitcast.12), channel_id=1, replica_groups=mesh['row'=4,'col'=32] {'row','col'}, use_global_device_ids=true, to_apply=%region_21.22 | all-reduce | flops 1 | bytes 8 | tf_op jit(solution)/shard_map/pmax | solution.py:96
  (27 shorter events, 0.2 us)
Async XLA Ops:
  7.2 132.4 %all-reduce.2.cloned.1.call-start = ((), (), s32[]{:S(2)}) async-start(), calls=%async_computation | async-start | bytes 2097152 | tf_op jit(solution)/shard_map/psum | solution.py:63
  21.4 7.9 %copy-start = (s32[256]{0:T(256)S(1)}, s32[256]{0:T(256)}, u32[]{:S(2)}) copy-start(s32[256]{0:T(256)} %param.7) | copy-start | bytes 3076
  21.4 8.0 %copy-start.2 = (s32[256]{0:T(256)S(1)}, s32[256]{0:T(256)}, u32[]{:S(2)}) copy-start(s32[256]{0:T(256)} %param.8) | copy-start | bytes 3076
  21.4 9.9 %copy-start.1 = (s32[256,16]{0,1:T(8,128)S(1)}, s32[256,16]{0,1:T(8,128)}, u32[]{:S(2)}) copy-start(s32[256,16]{0,1:T(8,128)} %param.9) | copy-start | bytes 49156
Sparse Core Ops, SparseCore 0:
  29.4 110.0 all-reduce.1
where the time goes:
time: 231 us
  waiting for transfers between devices  108 us (47%)
  blocking collectives  76.5 us (33%)
  other arithmetic  17.2 us (7%)
  between operations  14.3 us (6%)
  matrix products  10.3 us (4%)
  local copies, waits for them, and re-layouts  4.54 us (2%)
    psum x1, waiting for transfers between devices, local(): summed = lax.psum(partial_value, 'col')  108 us
    pmax x1, blocking collectives, local(): worst = lax.pmax(local_worst, ('row', 'col'))  65.5 us
    all_gather x1, blocking collectives, local(): piece = lax.all_gather(sample_cols, 'row', axis=0, tiled=True)  10.9 us
    dot_general x1, matrix products, local(): partial_value = jnp.dot(kept, piece, preferred_element_type=jnp.float32)  7.88 us
    another operation x4, other arithmetic, local(): factor = jnp.linalg.cholesky(gram)  6.03 us
    another operation x3, other arithmetic, local(): jax.scipy.linalg.cho_solve((lower, True), identity)  5 us
  transfers between devices with their start and end apart: 1, of which 1 were waited for; matrix products, arithmetic and copies ran while one was open for 1% of the time, Pallas kernels for 0%

commit v1 on v0

--- a/solution.py
+++ b/solution.py
@@ -60,7 +60,9 @@
     )
     local_row = jnp.clip(local_row, 0, group_rows - 1)
     valid_float = valid[:, None].astype(jnp.float32)
-    summed = lax.psum(partial_value, "col")
+    summed = partial_value
+    for hop in (1, 2, 4, 8, 16):
+        summed = summed + lax.ppermute(summed, "col", [(dev, dev ^ hop) for dev in range(32)])
     mine = jnp.take(summed, local_row, axis=0) * valid_float
     select = owned[None, :] & (rank[None, :] == jnp.arange(LEAF_MOST, dtype=jnp.int32)[:, None])
     select_int = select.astype(jnp.int32)

time: 231 us -> 211 us (0.913)
  waiting for transfers between devices: 108 us -> 88 us
  between operations: 14.3 us -> 0.9 us
  starting transfers between devices: 0.04 us -> 12.7 us
    psum x1 -> x0, waiting for transfers between devices: 108 us -> none  [local(): summed = lax.psum(partial_value, 'col')]
    ppermute x0 -> x5, waiting for transfers between devices: none -> 88 us  [local(): lax.ppermute(summed, 'col', [(dev, dev ^ hop) for dev in range(32)])]
    ppermute x0 -> x5, starting transfers between devices: none -> 12.7 us  [local(): lax.ppermute(summed, 'col', [(dev, dev ^ hop) for dev in range(32)])]
  transfers between devices with their start and end apart: 1 -> 5, of which waited for: 1 -> 5; matrix products, arithmetic and copies ran while one was open for 1% -> 1% of each run, Pallas kernels for 0% -> 0%
where the time goes in v1:
time: 211 us
  waiting for transfers between devices  88 us (42%)
  blocking collectives  78.4 us (37%)
  other arithmetic  17.8 us (8%)
  starting transfers between devices  12.7 us (6%)
  matrix products  9.86 us (5%)
  local copies, waits for them, and re-layouts  3.3 us (2%)
    ppermute x5, waiting for transfers between devices, local(): lax.ppermute(summed, 'col', [(dev, dev ^ hop) for dev in range(32)])  88 us
    pmax x1, blocking collectives, local(): worst = lax.pmax(local_worst, ('row', 'col'))  67.5 us
    ppermute x5, starting transfers between devices, local(): lax.ppermute(summed, 'col', [(dev, dev ^ hop) for dev in range(32)])  12.7 us
    all_gather x1, blocking collectives, local(): piece = lax.all_gather(sample_cols, 'row', axis=0, tiled=True)  10.9 us
    dot_general x1, matrix products, local(): partial_value = jnp.dot(kept, piece, preferred_element_type=jnp.float32)  7.47 us
    another operation x4, other arithmetic, local(): factor = jnp.linalg.cholesky(gram)  6.03 us
    another operation x3, other arithmetic, local(): jax.scipy.linalg.cho_solve((lower, True), identity)  5 us
  transfers between devices with their start and end apart: 5, of which 5 were waited for; matrix products, arithmetic and copies ran while one was open for 1% of the time, Pallas kernels for 0%

profile of v1, /device:TPU:1, one launch (start us, length us, event | category | flops | bytes accessed | tf_op | source)
XLA Modules:
  0.0 211.1 jit_solution(13716313358438469923)
XLA Ops:
  0.7 2.0 convert_reduce_fusion
  2.7 1.2 convert_reduce_fusion.1
  3.9 10.9 %all_gather.3 = bf16[1536,64]{0,1:T(8,128)(2,1)S(1)} all-gather(bf16[384,64]{0,1:T(8,128)(2,1)} %param.6), channel_id=1, replica_groups=mesh['row'=4,'col'=32] {'row'}, dimensions={0}, use_global_device_ids=true | all-gather | bytes 245760 | tf_op jit(solution)/shard_map/all_gather | solution.py:30
  14.8 7.5 %fusion = f32[4096,64]{0,1:T(8,128)S(1)} fusion(bf16[1536,64]{0,1:T(8,128)(2,1)S(1)} %all_gather.3, bf16[4096,1536]{1,0:T(8,128)(2,1)} %param.5, s32[1536]{0:T(1024)S(1)} %broadcast_add_fusion.1, s32[4096]{0:T(1024)S(1)} %broadcast_add_fusion, pred[1536]{0:T(1024)(128)(4,1)S(1)} %broadcast_compare_fusion), kind=kOutput, calls=%fused_computation.3 | convolution fusion | flops 824180736 | bytes 13852160 | tf_op jit(solution)/shard_map/dot_general | solution.py:36
  22.3 3.6 %collective-permute-start = (f32[4096,64]{0,1:T(8,128)S(1)}, f32[4096,64]{0,1:T(8,128)S(1)}, u32[]{:S(2)}, u32[]{:S(2)}) collective-permute-start(f32[4096,64]{0,1:T(8,128)S(1)} %fusion), channel_id=1, source_target_pairs={{0,1},{1,0},{2,3},{3,2},{4,5},{5,4},{6,7},{7,6},{8,9},{9,8},{10,11... | collective-permute-start | bytes 3145736 | tf_op jit(solution)/shard_map/ppermute | solution.py:65
  25.9 2.3 %collective-permute-done = f32[4096,64]{0,1:T(8,128)S(1)} collective-permute-done((f32[4096,64]{0,1:T(8,128)S(1)}, f32[4096,64]{0,1:T(8,128)S(1)}, u32[]{:S(2)}, u32[]{:S(2)}) %collective-permute-start) | collective-permute-done | bytes 1048608 | tf_op jit(solution)/shard_map/ppermute | solution.py:65
  28.1 0.2 add.148
  28.3 1.7 collective-permute-start.1
  30.4 0.1 fusion.11
  30.5 0.1 reduce_window_sum.17
  30.6 22.5 %collective-permute-done.1 = f32[4096,64]{0,1:T(8,128)S(1)} collective-permute-done((f32[4096,64]{0,1:T(8,128)S(1)}, f32[4096,64]{0,1:T(8,128)S(1)}, u32[]{:S(2)}, u32[]{:S(2)}) %collective-permute-start.1) | collective-permute-done | bytes 1048608 | tf_op jit(solution)/shard_map/ppermute | solution.py:65
  53.1 0.1 add.149
  53.2 3.3 %collective-permute-start.2 = (f32[4096,64]{0,1:T(8,128)S(1)}, f32[4096,64]{0,1:T(8,128)S(1)}, u32[]{:S(2)}, u32[]{:S(2)}) collective-permute-start(f32[4096,64]{0,1:T(8,128)S(1)} %add.149), channel_id=1, source_target_pairs={{0,4},{1,5},{2,6},{3,7},{4,0},{5,1},{6,2},{7,3},{8,12},{9,13},{10,... | collective-permute-start | bytes 3145736 | tf_op jit(solution)/shard_map/ppermute | solution.py:65
  56.5 0.1 fusion.10
  56.6 0.1 reduce_window_sum.18
  56.8 0.3 select_reduce_fusion.2
  57.3 0.1 fusion.33
  57.4 0.1 multiply_reduce_fusion.3
  57.6 21.3 %collective-permute-done.2 = f32[4096,64]{0,1:T(8,128)S(1)} collective-permute-done((f32[4096,64]{0,1:T(8,128)S(1)}, f32[4096,64]{0,1:T(8,128)S(1)}, u32[]{:S(2)}, u32[]{:S(2)}) %collective-permute-start.2) | collective-permute-done | bytes 1048608 | tf_op jit(solution)/shard_map/ppermute | solution.py:65
  78.8 0.1 add.150
  78.9 1.3 collective-permute-start.3
  80.3 0.1 fusion.19
  80.5 0.2 select_reduce_fusion
  80.8 21.2 %collective-permute-done.3 = f32[4096,64]{0,1:T(8,128)S(1)} collective-permute-done((f32[4096,64]{0,1:T(8,128)S(1)}, f32[4096,64]{0,1:T(8,128)S(1)}, u32[]{:S(2)}, u32[]{:S(2)}) %collective-permute-start.3) | collective-permute-done | bytes 1048608 | tf_op jit(solution)/shard_map/ppermute | solution.py:65
  101.9 0.1 add.151
  102.1 2.8 %collective-permute-start.4 = (f32[4096,64]{0,1:T(8,128)S(1)}, f32[4096,64]{0,1:T(8,128)S(1)}, u32[]{:S(2)}, u32[]{:S(2)}) collective-permute-start(f32[4096,64]{0,1:T(8,128)S(1)} %add.151), channel_id=1, source_target_pairs={{0,16},{1,17},{2,18},{3,19},{4,20},{5,21},{6,22},{7,23},{8,24},{9,... | collective-permute-start | bytes 3145736 | tf_op jit(solution)/shard_map/ppermute | solution.py:65
  105.0 20.8 %collective-permute-done.4 = f32[4096,64]{0,1:T(8,128)S(1)} collective-permute-done((f32[4096,64]{0,1:T(8,128)S(1)}, f32[4096,64]{0,1:T(8,128)S(1)}, u32[]{:S(2)}, u32[]{:S(2)}) %collective-permute-start.4) | collective-permute-done | bytes 1048608 | tf_op jit(solution)/shard_map/ppermute | solution.py:65
  125.8 0.1 add.152
  125.9 0.6 copy.23
  126.5 0.7 gather_fusion
  127.3 0.1 select_multiply_fusion
  127.4 0.6 gather_fusion.1
  128.0 0.3 fusion.8
  128.3 0.3 fusion.18
  128.6 0.1 fusion.48
  128.9 5.9 %custom-call.11 = f32[4,16,16]{2,1,0:T(8,128)S(1)} custom-call(f32[4,16,16]{2,1,0:T(8,128)S(1)} %fusion.17), custom_call_target="Cholesky" | custom-call | tf_op jit(solution)/shard_map/jit(cholesky)/cholesky | solution.py:82
  134.8 0.1 compare_reduce_fusion
  135.0 4.9 %custom-call.12 = f32[4,1,16,16]{2,3,1,0:T(8,128)S(1)} custom-call(f32[4,1,16,16]{3,2,1,0:T(8,128)S(1)} %select_bitcast_fusion), custom_call_target="InvertDiagBlocksLowerTriangular" | custom-call | tf_op jit(solution)/shard_map/vmap(jit(_cho_solve))/triangular_solve | solution.py:83
  139.9 0.3 fusion.14
  140.2 0.2 fusion.12
  140.4 0.8 multiply_reduce_fusion.2
  141.2 0.5 fusion.5
  141.7 0.1 copy.27
  141.8 0.3 multiply_reduce_fusion.1
  142.1 0.2 select_reduce_fusion.6
  142.2 0.6 fusion.36
  142.9 67.5 %pmax.7 = f32[1]{0:T(128)} all-reduce(f32[1]{0:T(128)} %bitcast.12), channel_id=1, replica_groups=mesh['row'=4,'col'=32] {'row','col'}, use_global_device_ids=true, to_apply=%region_20.21 | all-reduce | flops 1 | bytes 8 | tf_op jit(solution)/shard_map/pmax | solution.py:98
  210.4 0.7 copy.28
  (39 shorter events, 1.0 us)
Async XLA Ops:
  14.8 15.2 %copy-start = (s32[256]{0:T(256)S(1)}, s32[256]{0:T(256)}, u32[]{:S(2)}) copy-start(s32[256]{0:T(256)} %param.7) | copy-start | bytes 3076
  14.8 15.5 %copy-start.2 = (s32[256]{0:T(256)S(1)}, s32[256]{0:T(256)}, u32[]{:S(2)}) copy-start(s32[256]{0:T(256)} %param.8) | copy-start | bytes 3076
  22.3 35.1 %copy-start.1 = (s32[256,16]{0,1:T(8,128)S(1)}, s32[256,16]{0,1:T(8,128)}, u32[]{:S(2)}) copy-start(s32[256,16]{0,1:T(8,128)} %param.9) | copy-start | bytes 49156
  22.3 5.9 %collective-permute-start = (f32[4096,64]{0,1:T(8,128)S(1)}, f32[4096,64]{0,1:T(8,128)S(1)}, u32[]{:S(2)}, u32[]{:S(2)}) collective-permute-start(f32[4096,64]{0,1:T(8,128)S(1)} %fusion), channel_id=1, source_target_pairs={{0,1},{1,0},{2,3},{3,2},{4,5},{5,4},{6,7},{7,6},{8,9},{9,8},{10,11... | collective-permute-start | bytes 3145736 | tf_op jit(solution)/shard_map/ppermute | solution.py:65
  28.3 24.8 %collective-permute-start.1 = (f32[4096,64]{0,1:T(8,128)S(1)}, f32[4096,64]{0,1:T(8,128)S(1)}, u32[]{:S(2)}, u32[]{:S(2)}) collective-permute-start(f32[4096,64]{0,1:T(8,128)S(1)} %add.148), channel_id=1, source_target_pairs={{0,2},{1,3},{2,0},{3,1},{4,6},{5,7},{6,4},{7,5},{8,10},{9,11},{10,... | collective-permute-start | bytes 3145736 | tf_op jit(solution)/shard_map/ppermute | solution.py:65
  53.2 25.6 %collective-permute-start.2 = (f32[4096,64]{0,1:T(8,128)S(1)}, f32[4096,64]{0,1:T(8,128)S(1)}, u32[]{:S(2)}, u32[]{:S(2)}) collective-permute-start(f32[4096,64]{0,1:T(8,128)S(1)} %add.149), channel_id=1, source_target_pairs={{0,4},{1,5},{2,6},{3,7},{4,0},{5,1},{6,2},{7,3},{8,12},{9,13},{10,... | collective-permute-start | bytes 3145736 | tf_op jit(solution)/shard_map/ppermute | solution.py:65
  78.9 23.0 %collective-permute-start.3 = (f32[4096,64]{0,1:T(8,128)S(1)}, f32[4096,64]{0,1:T(8,128)S(1)}, u32[]{:S(2)}, u32[]{:S(2)}) collective-permute-start(f32[4096,64]{0,1:T(8,128)S(1)} %add.150), channel_id=1, source_target_pairs={{0,8},{1,9},{2,10},{3,11},{4,12},{5,13},{6,14},{7,15},{8,0},{9,1},... | collective-permute-start | bytes 3145736 | tf_op jit(solution)/shard_map/ppermute | solution.py:65
  102.1 23.8 %collective-permute-start.4 = (f32[4096,64]{0,1:T(8,128)S(1)}, f32[4096,64]{0,1:T(8,128)S(1)}, u32[]{:S(2)}, u32[]{:S(2)}) collective-permute-start(f32[4096,64]{0,1:T(8,128)S(1)} %add.151), channel_id=1, source_target_pairs={{0,16},{1,17},{2,18},{3,19},{4,20},{5,21},{6,22},{7,23},{8,24},{9,... | collective-permute-start | bytes 3145736 | tf_op jit(solution)/shard_map/ppermute | solution.py:65
